TPU v7x, 32 devices: a whole 2x2x4 slice. The times are simulated.
32 devices in a mesh: dom: 16 (over z, y, core), feat: 2 (over x).
Axes of the slice: x: 2, y: 2, z: 4, core: 2. Of those that a mesh axis runs over, the one named last changes fastest.
Arguments:
- features: bfloat16 [256, 8192], P('feat', 'dom'), may hold values from -6 to 6
- in_degree: int32 [8192], P('dom'), may hold values from 16 to 64
- send_rows: int32 [16, 16, 16], P('dom'), may hold values from 0 to 511
- send_count: int32 [16, 16], P('dom'), may hold values from 0 to 16, as said below
- hub_owner: int32 [4], replicated, may hold values from 0 to 15, as said below
- hub_rows: int32 [4, 128], replicated, may hold values from 0 to 511
- local_dest: int32 [256], P('dom'), may hold values from 0 to 3
- local_source: int32 [256], P('dom'), may hold values from 0 to 3
- local_tiles: bfloat16 [256, 128, 128], P('dom'), may hold values from 0 to 1
- border_dest: int32 [256], P('dom'), may hold values from 0 to 3
- border_source: int32 [256], P('dom'), may hold values from 0 to 1
- border_tiles: bfloat16 [256, 128, 128], P('dom'), may hold values from 0 to 1
- hub_dest: int32 [256], P('dom'), may hold values from 0 to 3
- hub_source: int32 [256], P('dom'), may hold values from 0 to 3
- hub_tiles: bfloat16 [256, 128, 128], P('dom'), may hold values from 0 to 1
- self_weight: bfloat16 [256, 256], P('feat'), may hold values from -0.375 to 0.375
- neighbor_weight: bfloat16 [256, 256], P('feat'), may hold values from -0.375 to 0.375
- out_bias: float32 [256], P('feat'), may hold values from -3 to 3
Outputs:
- updated: bfloat16 [256, 8192], P('feat', 'dom')
Inputs may be any that keep to these rules, and one draw needn't show every extreme that they name: send_count[q, p] of the 16 slots from q to p are live; in every draw some destinations receive 16 live rows from every source. Hub block b belongs to partition hub_owner[b]; one partition owns exactly 2 blocks, every other partition at most one.
All inputs are finite; a program needn't handle non-finite values.
Results may differ from a plain program's by a relative error of at most 0.0034.
Values may be sent and summed in bfloat16 or wider, within the bound.
No kernel may reach another device: no remote copies, remote signals or barrier semaphores. Data moves between devices by JAX's collectives and lax.ppermute only.
A program may use at most 64 MiB of HBM per device.

v0:
```python
import jax
import jax.numpy as jnp
from jax import lax
from jax.sharding import PartitionSpec as P

HOWN = 2


def tile_terms(blocks, targets, source, tile_values, row_blocks):
    picked = jnp.take(blocks, source, axis=1)
    partial_value = jnp.einsum(
        "ftk,tik->fti", picked, tile_values, preferred_element_type=jnp.float32
    )
    onehot = (targets[:, None] == jnp.arange(row_blocks, dtype=jnp.int32)[None, :]).astype(
        jnp.float32
    )
    return jnp.einsum("fti,tr->fri", partial_value, onehot, precision=lax.Precision.HIGHEST)


def shards(
    features,
    in_degree,
    send_rows,
    send_count,
    hub_owner,
    hub_rows,
    local_dest,
    local_source,
    local_tiles,
    border_dest,
    border_source,
    border_tiles,
    hub_dest,
    hub_source,
    hub_tiles,
    self_weight,
    neighbor_weight,
    out_bias,
):
    feat_rows, vertex_count = features.shape
    tile_size = local_tiles.shape[1]
    row_blocks = vertex_count // tile_size
    partitions = lax.axis_size("dom")
    capacity = send_rows.shape[2]
    own_blocks = features.reshape(feat_rows, row_blocks, tile_size)
    local_sum = tile_terms(own_blocks, local_dest, local_source, local_tiles, row_blocks)
    pick_rows = send_rows[0].reshape(-1)
    outgoing = jnp.take(features, pick_rows, axis=1).reshape(feat_rows, partitions, capacity)
    alive_slots = (jnp.arange(capacity, dtype=jnp.int32)[None, :] < send_count[0][:, None]).astype(
        jnp.bfloat16
    )
    outgoing = outgoing * alive_slots[None]
    incoming = lax.all_to_all(outgoing, "dom", split_axis=1, concat_axis=1, tiled=True)
    border_blocks = incoming.reshape(feat_rows, partitions * capacity // tile_size, tile_size)
    border_sum = tile_terms(border_blocks, border_dest, border_source, border_tiles, row_blocks)
    hub_count = hub_owner.shape[0]
    position = lax.axis_index("dom")
    block_ids = jnp.arange(hub_count, dtype=jnp.int32)
    earlier = block_ids[:, None] > block_ids[None, :]
    same_owner = hub_owner[:, None] == hub_owner[None, :]
    order_rank = jnp.sum((earlier & same_owner).astype(jnp.int32), axis=1)
    owned_here = hub_owner == position
    choose = (
        owned_here[None, :] & (order_rank[None, :] == jnp.arange(HOWN, dtype=jnp.int32)[:, None])
    ).astype(jnp.int32)
    slot_rows = jnp.sum(choose[:, :, None] * hub_rows[None], axis=1)
    owned_blocks = jnp.take(features, slot_rows.reshape(-1), axis=1).reshape(
        feat_rows, HOWN, tile_size
    )
    everyone = lax.all_gather(owned_blocks, "dom", axis=1, tiled=True)
    hub_blocks = jnp.take(everyone, hub_owner * HOWN + order_rank, axis=1)
    hub_sum = tile_terms(hub_blocks, hub_dest, hub_source, hub_tiles, row_blocks)
    degree = in_degree.astype(jnp.float32).reshape(row_blocks, tile_size)
    aggregate = (
        ((local_sum + border_sum + hub_sum) / degree[None])
        .astype(jnp.bfloat16)
        .reshape(feat_rows, vertex_count)
    )
    running = jnp.dot(
        self_weight,
        lax.all_gather(features, "feat", axis=0, tiled=True),
        preferred_element_type=jnp.float32,
    )
    combined = running + jnp.dot(
        neighbor_weight,
        lax.all_gather(aggregate, "feat", axis=0, tiled=True),
        preferred_element_type=jnp.float32,
    )
    return jnp.maximum(combined + out_bias[:, None], 0.0).astype(jnp.bfloat16)


def solution(mesh):
    placed = (
        P("feat", "dom"),
        P("dom"),
        P("dom", None, None),
        P("dom", None),
        P(),
        P(),
        P("dom"),
        P("dom"),
        P("dom", None, None),
        P("dom"),
        P("dom"),
        P("dom", None, None),
        P("dom"),
        P("dom"),
        P("dom", None, None),
        P("feat", None),
        P("feat", None),
        P("feat"),
    )
    return jax.shard_map(
        shards, mesh=mesh, in_specs=placed, out_specs=P("feat", "dom"), check_vma=False
    )
```

profile of v0, /device:TPU:0, one launch (start us, length us, event | category | flops | bytes accessed | tf_op | source)
XLA Modules:
  0.0 80.8 jit_solution(9627374421501627303)
XLA Ops:
  6.5 0.0 copy-start
  6.5 0.8 %reshape_squeeze.3 = s32[256]{0:T(256)S(1)} reshape(s32[1,16,16]{2,1,0:T(8,128)} %param.24) | data formatting | bytes 2048 | tf_op jit(solution)/shard_map/reshape;squeeze | solution.py:47
  7.4 1.0 %copy.61 = bf16[128,512]{0,1:T(8,128)(2,1)S(1)} copy(bf16[128,512]{1,0:T(8,128)(2,1)} %param.22) | data formatting | bytes 262144 | tf_op args[0]
  8.4 0.0 copy-start.11
  8.4 0.6 copy-done.11
  9.1 0.1 fusion.21
  9.2 0.9 %gather_fusion.3 = bf16[256,128]{1,0:T(8,128)(2,1)S(1)} fusion(bf16[128,512]{0,1:T(8,128)(2,1)S(1)} %copy.61, s32[1024]{0:T(1024)S(1)} %pad_clamp_fusion.4), kind=kCustom, calls=%fused_computation.1.clone | custom fusion | bytes 132096 | tf_op jit(solution)/shard_map/jit(_take)/gather | solution.py:48
  10.0 0.1 broadcast_select_fusion.1
  10.1 0.7 broadcast_multiply_fusion
  10.9 7.4 %all-to-all-start = ((bf16[128,16,16]{0,2,1:T(8,128)(2,1)}), bf16[128,16,16]{0,2,1:T(8,128)(2,1)S(1)}, u32[]{:S(2)}, u32[]{:S(2)}) async-start(bf16[128,16,16]{0,2,1:T(8,128)(2,1)} %broadcast_multiply_fusion), calls=%async_computation | async-start | bytes 131072 | tf_op jit(solution)/shard_map/all_to_all | solution.py:53
  18.3 0.0 copy-start.12
  18.3 0.0 all-gather.2.cloned.1.call-start
  18.3 0.6 copy-done.12
  18.9 0.2 convert_reduce_fusion
  19.1 0.0 copy-start.6
  19.1 0.7 copy-done.6
  19.8 0.1 multiply_reduce_fusion
  19.9 0.9 %gather_fusion.4 = bf16[256,128]{1,0:T(8,128)(2,1)S(1)} fusion(bf16[128,512]{0,1:T(8,128)(2,1)S(1)} %copy.61, s32[1024]{0:T(1024)S(1)} %pad_clamp_fusion.2), kind=kCustom, calls=%fused_computation.3.clone | custom fusion | bytes 132096 | tf_op jit(solution)/shard_map/jit(_take)/gather | solution.py:67
  20.8 0.1 broadcast_select_fusion
  20.9 0.7 copy.68
  21.6 0.0 copy-start.13
  21.6 0.0 all-gather.2.cloned.1.call-update
  21.6 0.6 copy-done.13
  22.3 0.0 copy-start.14
  22.3 0.6 copy-done.14
  23.0 0.1 copy.62
  23.1 0.0 copy-start.15
  23.1 0.6 gather_fusion.2
  23.8 0.0 copy-done.15
  23.8 0.0 copy-start.7
  23.8 0.6 copy-done.7
  24.5 0.0 copy-done
  24.5 0.0 copy-start.8
  24.5 0.5 convolution_bitcast_fusion.2
  25.0 0.1 copy-done.8
  25.1 0.0 copy-start.3
  25.1 1.1 %fusion.7 = f32[4,128,128]{2,0,1:T(4,128)S(1)} fusion(f32[128,16,128]{2,0,1:T(8,128)S(1)} %convolution_bitcast_fusion.2, s32[16]{0:T(128)S(1)} %copy-done.8), kind=kOutput, calls=%fused_computation.20 | convolution fusion | flops 12582976 | bytes 1310784 | tf_op jit(solution)/shard_map/fti,tr->fri/dot_general | solution.py:17
  26.2 0.0 copy-done.3
  26.2 6.5 %all_gather.9 = bf16[256,512]{1,0:T(8,128)(2,1)S(1)} all-gather(bf16[128,512]{1,0:T(8,128)(2,1)S(1)} %copy-done.3), channel_id=1, replica_groups=mesh['dom'=16,'feat'=2] {'feat'}, dimensions={0}, use_global_device_ids=true | all-gather | bytes 393216 | tf_op jit(solution)/shard_map/all_gather | solution.py:81
  32.7 0.0 all-to-all-done
  32.7 0.1 copy.65
  32.9 0.0 copy-start.1
  32.9 0.6 gather_fusion
  33.5 0.4 copy-done.1
  33.9 0.0 copy-start.9
  33.9 0.5 convolution_bitcast_fusion.1
  34.4 0.1 copy-done.9
  34.6 1.1 %convolution_add_fusion.1 = f32[4,128,128]{2,0,1:T(4,128)S(1)} fusion(f32[4,128,128]{2,0,1:T(4,128)S(1)} %fusion.7, f32[128,16,128]{2,0,1:T(8,128)S(1)} %convolution_bitcast_fusion.1, s32[16]{0:T(128)S(1)} %copy-done.9), kind=kOutput, calls=%fused_computation.10 | convolution fusion | flops 12648512 | bytes 1572928 | tf_op jit(solution)/shard_map/fti,tr->fri/dot_general | solution.py:17
  35.6 25.4 %all-gather.2.cloned.1.call-done = bf16[128,32,128]{2,0,1:T(8,128)(2,1)} async-done(((bf16[128,2,128]{2,0,1:T(8,128)(2,1)}), bf16[128,32,128]{2,0,1:T(8,128)(2,1)}) %all-gather.2.cloned.1.call-update) | async-done | bytes 1048592 | tf_op jit(solution)/shard_map/all_gather | solution.py:70
  61.0 1.8 %gather_fusion.1 = bf16[4,128,128]{2,1,0:T(8,128)(2,1)S(1)} fusion(bf16[128,32,128]{2,0,1:T(8,128)(2,1)} %all-gather.2.cloned.1.call-done, s32[1024]{0:T(1024)S(1)} %pad_clamp_fusion.1), kind=kCustom, calls=%fused_computation.5 | custom fusion | bytes 262160 | tf_op jit(solution)/shard_map/jit(_take)/gather | solution.py:71
  62.8 0.1 select_bitcast_fusion
  62.9 0.0 copy-start.2
  62.9 0.6 gather_fusion.5
  63.6 0.4 copy-done.2
  64.0 0.5 convolution_bitcast_fusion
  64.5 0.1 copy-done.16
  64.6 1.1 %fusion.3 = bf16[4,128,128]{2,0,1:T(4,128)(2,1)S(1)} fusion(f32[4,128,128]{2,0,1:T(4,128)S(1)} %convolution_add_fusion.1, f32[128,16,128]{2,0,1:T(8,128)S(1)} %convolution_bitcast_fusion, f32[4,128]{1,0:T(4,128)S(1)} %convert_bitcast_fusion, s32[16]{0:T(128)S(1)} %copy-done.16), kind=kOutput, calls=%fused_computation.16 | convolution fusion | flops 12779584 | bytes 1443904 | tf_op jit(solution)/shard_map/fti,tr->fri/dot_general | solution.py:17
  65.7 0.0 copy-start.4
  65.7 6.5 %all_gather.11 = bf16[256,512]{1,0:T(8,128)(2,1)S(1)} all-gather(bf16[128,512]{1,0:T(8,128)(2,1)S(1)} %bitcast.56), channel_id=1, replica_groups=mesh['dom'=16,'feat'=2] {'feat'}, dimensions={0}, use_global_device_ids=true | all-gather | bytes 393216 | tf_op jit(solution)/shard_map/all_gather | solution.py:86
  72.2 0.0 copy-done.4
  72.2 0.2 convolution_bitcast_fusion.3
  72.4 0.6 copy-done.5
  73.1 0.0 copy-done.10
  73.1 0.8 %fusion.4 = bf16[128,512]{1,0:T(8,128)(2,1)} fusion(f32[128,512]{1,0:T(8,128)S(1)} %convolution_bitcast_fusion.3, bf16[128,256]{1,0:T(8,128)(2,1)S(1)} %copy-done.5, bf16[256,512]{1,0:T(8,128)(2,1)S(1)} %all_gather.9, f32[128]{0:T(128)S(1)} %copy-done.10), kind=kOutput, calls=%fused_computation.17 | convolution fusion | flops 33816576 | bytes 721408 | tf_op jit(solution)/shard_map/dot_general | solution.py:79
  (23 shorter events, 0.1 us)
Async XLA Ops:
  6.5 17.9 %copy-start = (bf16[16,128,128]{2,1,0:T(8,128)(2,1)S(1)}, bf16[16,128,128]{2,1,0:T(8,128)(2,1)}, u32[]{:S(2)}) copy-start(bf16[16,128,128]{2,1,0:T(8,128)(2,1)} %param.30) | copy-start | bytes 1572868
  8.4 0.7 copy-start.11
  10.9 21.9 %all-to-all-start = ((bf16[128,16,16]{0,2,1:T(8,128)(2,1)}), bf16[128,16,16]{0,2,1:T(8,128)(2,1)S(1)}, u32[]{:S(2)}, u32[]{:S(2)}) async-start(bf16[128,16,16]{0,2,1:T(8,128)(2,1)} %broadcast_multiply_fusion), calls=%async_computation | async-start | bytes 131072 | tf_op jit(solution)/shard_map/all_to_all | solution.py:53
  18.3 0.7 copy-start.12
  18.3 42.8 %all-gather.2.cloned.1.call-start = ((), (), s32[]{:S(2)}) async-start(), calls=%async_computation.1 | async-start | bytes 1114112 | tf_op jit(solution)/shard_map/all_gather | solution.py:70
  19.1 0.7 copy-start.6
  21.6 0.7 copy-start.13
  22.3 0.7 copy-start.14
  23.1 0.7 copy-start.15
  23.8 0.7 copy-start.7
  24.5 0.7 copy-start.8
  25.1 1.1 %copy-start.3 = (bf16[128,512]{1,0:T(8,128)(2,1)S(1)}, bf16[128,512]{1,0:T(8,128)(2,1)}, u32[]{:S(2)}) copy-start(bf16[128,512]{1,0:T(8,128)(2,1)} %param.22) | copy-start | bytes 393220
  32.9 1.0 %copy-start.1 = (bf16[16,128,128]{2,1,0:T(8,128)(2,1)S(1)}, bf16[16,128,128]{2,1,0:T(8,128)(2,1)}, u32[]{:S(2)}) copy-start(bf16[16,128,128]{2,1,0:T(8,128)(2,1)} %param.33) | copy-start | bytes 1572868
  33.9 0.7 copy-start.9
  62.9 1.0 %copy-start.2 = (bf16[16,128,128]{2,1,0:T(8,128)(2,1)S(1)}, bf16[16,128,128]{2,1,0:T(8,128)(2,1)}, u32[]{:S(2)}) copy-start(bf16[16,128,128]{2,1,0:T(8,128)(2,1)} %param.36) | copy-start | bytes 1572868
  64.0 0.7 copy-start.16
  65.7 6.5 %copy-start.4 = (bf16[128,256]{1,0:T(8,128)(2,1)S(1)}, bf16[128,256]{1,0:T(8,128)(2,1)}, u32[]{:S(2)}) copy-start(bf16[128,256]{1,0:T(8,128)(2,1)} %param.38) | copy-start | bytes 196612
  72.2 0.8 %copy-start.5 = (bf16[128,256]{1,0:T(8,128)(2,1)S(1)}, bf16[128,256]{1,0:T(8,128)(2,1)}, u32[]{:S(2)}) copy-start(bf16[128,256]{1,0:T(8,128)(2,1)} %param.37) | copy-start | bytes 196612
  72.2 0.8 %copy-start.10 = (f32[128]{0:T(128)S(1)}, f32[128]{0:T(128)}, u32[]{:S(2)}) copy-start(f32[128]{0:T(128)} %param.39) | copy-start | bytes 1540
Sparse Core Ops, SparseCore 0:
  21.7 39.2 all-gather.1
where the time goes:
time: 81.3 us; the launch traced here: 80.8 us
  waiting for transfers between devices  25.4 us (31%)
  local copies, waits for them, and re-layouts  14 us (17%)
  between operations  13.7 us (17%)
  blocking collectives  13 us (16%)
  starting transfers between devices  7.43 us (9%)
  matrix products  5.75 us (7%)
  other arithmetic  1.48 us (2%)
    all_gather x1, waiting for transfers between devices, shards(): everyone = lax.all_gather(owned_blocks, 'dom', axis=1, tiled=True)  25.4 us
    all_to_all x1, starting transfers between devices, shards(): lax.all_to_all(outgoing, 'dom', split_axis=1, concat_axis=1, tiled=True)  7.38 us
    unnamed x36, local copies, waits for them, and re-layouts  6.71 us
    all_gather x1, blocking collectives, shards(): lax.all_gather(features, 'feat', axis=0, tiled=True)  6.51 us
    all_gather x1, blocking collectives, shards(): lax.all_gather(aggregate, 'feat', axis=0, tiled=True)  6.47 us
    dot_general x3, matrix products, tile_terms(): jnp.einsum('fti,tr->fri', partial_value, onehot, precision=lax.Precision....  3.16 us
    gather x3, local copies, waits for them, and re-layouts, tile_terms(): picked = jnp.take(blocks, source, axis=1)  1.94 us
    gather x1, local copies, waits for them, and re-layouts, shards(): hub_blocks = jnp.take(everyone, hub_owner * HOWN + order_rank, axis=1)  1.79 us
  transfers between devices with their start and end apart: 2, of which 1 were waited for; matrix products, arithmetic and copies ran while one was open for 8% of the time, Pallas kernels for 0%

commit v1 on v0

--- a/solution.py
+++ b/solution.py
@@ -67,7 +67,23 @@
     owned_blocks = jnp.take(features, slot_rows.reshape(-1), axis=1).reshape(
         feat_rows, HOWN, tile_size
     )
-    everyone = lax.all_gather(owned_blocks, "dom", axis=1, tiled=True)
+    slots = []
+    n_lanes = lax.psum(1, axis_name="dom")
+    for at in range(n_lanes):
+        slots.append((at, (at + 1) % n_lanes))
+    row_list = []
+    for at in range(n_lanes):
+        row_list.append((at, (at - 1) % n_lanes))
+    k_now, current_value = ([owned_blocks], [owned_blocks])
+    for _ in range(n_lanes // 2):
+        parts_out = lax.ppermute(k_now[-1], axis_name="dom", perm=slots)
+        k_now.append(parts_out)
+    for _ in range((n_lanes - 1) // 2):
+        w_next = lax.ppermute(current_value[-1], axis_name="dom", perm=row_list)
+        current_value.append(w_next)
+    passed = jnp.concatenate([*k_now[::-1], *current_value[1:]], axis=1)
+    view_out = lax.axis_index("dom")
+    everyone = jnp.roll(passed, shift=(view_out - n_lanes // 2) * owned_blocks.shape[1], axis=1)
     hub_blocks = jnp.take(everyone, hub_owner * HOWN + order_rank, axis=1)
     hub_sum = tile_terms(hub_blocks, hub_dest, hub_source, hub_tiles, row_blocks)
     degree = in_degree.astype(jnp.float32).reshape(row_blocks, tile_size)

time: 81.3 us -> 81.7 us (level)
  starting transfers between devices: 7.43 us -> 35.7 us
  between operations: 13.7 us -> 0.58 us
  waiting for transfers between devices: 25.4 us -> 15.5 us
  local copies, waits for them, and re-layouts: 14 us -> 7.06 us
  other arithmetic: 1.48 us -> 5.5 us
  blocking collectives: 13 us -> 11.3 us
    ppermute x0 -> x15, starting transfers between devices: none -> 32.1 us  [the longest x7 31.1 us: shards(): w_next = lax.ppermute(current_value[-1], axis_name='dom', perm=row_list)]
    all_gather x1 -> x0, waiting for transfers between devices: 25.4 us -> none  [shards(): everyone = lax.all_gather(owned_blocks, 'dom', axis=1, tiled=True)]
    ppermute x0 -> x15, waiting for transfers between devices: none -> 15.5 us  [the longest x8 11.6 us: shards(): parts_out = lax.ppermute(k_now[-1], axis_name='dom', perm=slots)]
    unnamed x36 -> x61, local copies, waits for them, and re-layouts: 6.71 us -> 1.56 us
    all_to_all x1, starting transfers between devices: 7.38 us -> 3.62 us  [shards(): lax.all_to_all(outgoing, 'dom', split_axis=1, concat_axis=1, tiled=True)]
    select_n x3, other arithmetic: 0.01 us -> 1.32 us  [tile_terms(): picked = jnp.take(blocks, source, axis=1)]
    gather x1, local copies, waits for them, and re-layouts: 1.79 us -> 0.57 us  [shards(): hub_blocks = jnp.take(everyone, hub_owner * HOWN + order_rank, axis=1)]
    all_gather x1, blocking collectives: 6.51 us -> 5.63 us  [shards(): lax.all_gather(features, 'feat', axis=0, tiled=True)]
  transfers between devices with their start and end apart: 2 -> 16, of which waited for: 1 -> 7; matrix products, arithmetic and copies ran while one was open for 8% -> 11% of each run, Pallas kernels for 0% -> 0%
where the time goes in v1:
time: 81.7 us; the launch traced here: 81.3 us
  starting transfers between devices  35.7 us (44%)
  waiting for transfers between devices  15.5 us (19%)
  blocking collectives  11.3 us (14%)
  local copies, waits for them, and re-layouts  7.06 us (9%)
  matrix products  5.75 us (7%)
  other arithmetic  5.5 us (7%)
    ppermute x7, starting transfers between devices, shards(): w_next = lax.ppermute(current_value[-1], axis_name='dom', perm=row_list)  31.1 us
    ppermute x8, waiting for transfers between devices, shards(): parts_out = lax.ppermute(k_now[-1], axis_name='dom', perm=slots)  11.6 us
    all_gather x1, blocking collectives, shards(): lax.all_gather(aggregate, 'feat', axis=0, tiled=True)  5.64 us
    all_gather x1, blocking collectives, shards(): lax.all_gather(features, 'feat', axis=0, tiled=True)  5.63 us
    ppermute x7, waiting for transfers between devices, shards(): w_next = lax.ppermute(current_value[-1], axis_name='dom', perm=row_list)  3.84 us
    all_to_all x1, starting transfers between devices, shards(): lax.all_to_all(outgoing, 'dom', split_axis=1, concat_axis=1, tiled=True)  3.62 us
    dot_general x3, matrix products, tile_terms(): jnp.einsum('fti,tr->fri', partial_value, onehot, precision=lax.Precision....  3.16 us
    gather x3, local copies, waits for them, and re-layouts, tile_terms(): picked = jnp.take(blocks, source, axis=1)  1.95 us
  transfers between devices with their start and end apart: 16, of which 7 were waited for; matrix products, arithmetic and copies ran while one was open for 11% of the time, Pallas kernels for 0%

profile of v1, /device:TPU:0, one launch (start us, length us, event | category | flops | bytes accessed | tf_op | source)
XLA Modules:
  0.0 81.3 jit_solution(16603174550052174920)
XLA Ops:
  0.0 0.9 %convert_reduce_fusion = s32[4]{0:T(128)S(1)} fusion(s32[4]{0:T(128)} %param.26), kind=kLoop, calls=%fused_computation.87 | loop fusion | flops 76 | bytes 32 | tf_op jit(solution)/shard_map/reduce_sum | solution.py:61
  0.9 0.7 compare_and_fusion.4
  1.6 0.8 multiply_reduce_fusion
  2.4 0.7 compare_select_fusion.2
  3.0 1.0 %copy.54 = bf16[128,512]{0,1:T(8,128)(2,1)S(1)} copy(bf16[128,512]{1,0:T(8,128)(2,1)} %param.22) | data formatting | bytes 262144 | tf_op args[0]
  4.1 0.9 %gather_fusion.4 = bf16[256,128]{1,0:T(8,128)(2,1)S(1)} fusion(bf16[128,512]{0,1:T(8,128)(2,1)S(1)} %copy.54, s32[1024]{0:T(1024)S(1)} %get-tuple-element.11), kind=kCustom, calls=%fused_computation.3.clone | custom fusion | bytes 132096 | tf_op jit(solution)/shard_map/jit(_take)/gather | solution.py:67
  4.9 0.1 broadcast_select_fusion
  5.0 0.1 copy.61
  5.2 0.5 collective-permute-start
  5.7 5.1 %collective-permute-start.8 = (bf16[128,2,128]{2,0,1:T(8,128)(2,1)S(1)}, bf16[128,2,128]{2,0,1:T(8,128)(2,1)S(1)}, u32[]{:S(2)}, u32[]{:S(2)}) collective-permute-start(bf16[128,2,128]{2,0,1:T(8,128)(2,1)S(1)} %copy.61), channel_id=1, source_target_pairs={{0,30},{2,0},{4,2},{6,4},{8,6},{10,8},{12,10},{14,12},{16,14},{18,... | collective-permute-start | bytes 196616 | tf_op jit(solution)/shard_map/ppermute | solution.py:82
  10.7 0.8 reshape_squeeze.3
  11.5 0.7 compare_select_fusion.3
  12.2 0.9 %gather_fusion.3 = bf16[256,128]{1,0:T(8,128)(2,1)S(1)} fusion(bf16[128,512]{0,1:T(8,128)(2,1)S(1)} %copy.54, s32[1024]{0:T(1024)S(1)} %get-tuple-element.12), kind=kCustom, calls=%fused_computation.1.clone | custom fusion | bytes 132096 | tf_op jit(solution)/shard_map/jit(_take)/gather | solution.py:48
  13.1 0.7 fusion.21
  13.8 0.1 broadcast_select_fusion.1
  13.9 0.7 broadcast_multiply_fusion
  14.6 3.6 %all-to-all-start = ((bf16[128,16,16]{0,2,1:T(8,128)(2,1)}), bf16[128,16,16]{0,2,1:T(8,128)(2,1)S(1)}, u32[]{:S(2)}, u32[]{:S(2)}) async-start(bf16[128,16,16]{0,2,1:T(8,128)(2,1)} %broadcast_multiply_fusion), calls=%async_computation | async-start | bytes 131072 | tf_op jit(solution)/shard_map/all_to_all | solution.py:53
  18.3 0.1 copy.55
  18.4 0.0 copy-start.11
  18.4 0.0 copy-start.12
  18.5 0.0 copy-start.3
  18.5 0.6 gather_fusion.2
  19.1 0.0 copy-start.1
  19.2 0.5 convolution_bitcast_fusion.2
  19.7 1.1 %fusion.7 = f32[4,128,128]{2,0,1:T(4,128)S(1)} fusion(f32[128,16,128]{2,0,1:T(8,128)S(1)} %convolution_bitcast_fusion.2, s32[16]{0:T(128)S(1)} %copy-done.7), kind=kOutput, calls=%fused_computation.20 | convolution fusion | flops 12582976 | bytes 1310784 | tf_op jit(solution)/shard_map/fti,tr->fri/dot_general | solution.py:17
  20.8 0.0 copy-start.8
  20.8 0.0 collective-permute-done
  20.8 0.5 collective-permute-start.1
  21.3 6.0 %collective-permute-done.1 = bf16[128,2,128]{2,0,1:T(8,128)(2,1)S(1)} collective-permute-done((bf16[128,2,128]{2,0,1:T(8,128)(2,1)S(1)}, bf16[128,2,128]{2,0,1:T(8,128)(2,1)S(1)}, u32[]{:S(2)}, u32[]{:S(2)}) %collective-permute-start.1) | collective-permute-done | bytes 65568 | tf_op jit(solution)/shard_map/ppermute | solution.py:79
  27.2 0.0 collective-permute-start.2
  27.3 4.5 %collective-permute-start.9 = (bf16[128,2,128]{2,0,1:T(8,128)(2,1)S(1)}, bf16[128,2,128]{2,0,1:T(8,128)(2,1)S(1)}, u32[]{:S(2)}, u32[]{:S(2)}) collective-permute-start(bf16[128,2,128]{2,0,1:T(8,128)(2,1)S(1)} %collective-permute-done.8), channel_id=1, source_target_pairs={{0,30},{2,0},{4,2},{6,4},{8,6},{10,8},{12,10},{14,12},{16,14},{18,... | collective-permute-start | bytes 196616 | tf_op jit(solution)/shard_map/ppermute | solution.py:82
  31.7 1.9 %collective-permute-done.2 = bf16[128,2,128]{2,0,1:T(8,128)(2,1)S(1)} collective-permute-done((bf16[128,2,128]{2,0,1:T(8,128)(2,1)S(1)}, bf16[128,2,128]{2,0,1:T(8,128)(2,1)S(1)}, u32[]{:S(2)}, u32[]{:S(2)}) %collective-permute-start.2) | collective-permute-done | bytes 65568 | tf_op jit(solution)/shard_map/ppermute | solution.py:79
  33.7 4.5 %collective-permute-start.10 = (bf16[128,2,128]{2,0,1:T(8,128)(2,1)S(1)}, bf16[128,2,128]{2,0,1:T(8,128)(2,1)S(1)}, u32[]{:S(2)}, u32[]{:S(2)}) collective-permute-start(bf16[128,2,128]{2,0,1:T(8,128)(2,1)S(1)} %collective-permute-done.9), channel_id=1, source_target_pairs={{0,30},{2,0},{4,2},{6,4},{8,6},{10,8},{12,10},{14,12},{16,14},{18,... | collective-permute-start | bytes 196616 | tf_op jit(solution)/shard_map/ppermute | solution.py:82
  38.1 1.9 %collective-permute-done.3 = bf16[128,2,128]{2,0,1:T(8,128)(2,1)S(1)} collective-permute-done((bf16[128,2,128]{2,0,1:T(8,128)(2,1)S(1)}, bf16[128,2,128]{2,0,1:T(8,128)(2,1)S(1)}, u32[]{:S(2)}, u32[]{:S(2)}) %collective-permute-start.3) | collective-permute-done | bytes 65568 | tf_op jit(solution)/shard_map/ppermute | solution.py:79
  40.0 0.0 collective-permute-done.10
  40.0 4.5 %collective-permute-start.11 = (bf16[128,2,128]{2,0,1:T(8,128)(2,1)S(1)}, bf16[128,2,128]{2,0,1:T(8,128)(2,1)S(1)}, u32[]{:S(2)}, u32[]{:S(2)}) collective-permute-start(bf16[128,2,128]{2,0,1:T(8,128)(2,1)S(1)} %collective-permute-done.10), channel_id=1, source_target_pairs={{0,30},{2,0},{4,2},{6,4},{8,6},{10,8},{12,10},{14,12},{16,14},{18,... | collective-permute-start | bytes 196616 | tf_op jit(solution)/shard_map/ppermute | solution.py:82
  44.5 1.9 %collective-permute-done.4 = bf16[128,2,128]{2,0,1:T(8,128)(2,1)S(1)} collective-permute-done((bf16[128,2,128]{2,0,1:T(8,128)(2,1)S(1)}, bf16[128,2,128]{2,0,1:T(8,128)(2,1)S(1)}, u32[]{:S(2)}, u32[]{:S(2)}) %collective-permute-start.4) | collective-permute-done | bytes 65568 | tf_op jit(solution)/shard_map/ppermute | solution.py:79
  46.4 5.6 %all_gather.6 = bf16[256,512]{1,0:T(8,128)(2,1)S(1)} all-gather(bf16[128,512]{1,0:T(8,128)(2,1)S(1)} %copy-done.3), channel_id=1, replica_groups=mesh['dom'=16,'feat'=2] {'feat'}, dimensions={0}, use_global_device_ids=true | all-gather | bytes 393216 | tf_op jit(solution)/shard_map/all_gather | solution.py:97
  52.1 0.1 copy.58
  52.2 0.7 gather_fusion
  52.9 3.6 %collective-permute-start.12 = (bf16[128,2,128]{2,0,1:T(8,128)(2,1)S(1)}, bf16[128,2,128]{2,0,1:T(8,128)(2,1)S(1)}, u32[]{:S(2)}, u32[]{:S(2)}) collective-permute-start(bf16[128,2,128]{2,0,1:T(8,128)(2,1)S(1)} %collective-permute-done.11), channel_id=1, source_target_pairs={{0,30},{2,0},{4,2},{6,4},{8,6},{10,8},{12,10},{14,12},{16,14},{18,... | collective-permute-start | bytes 196616 | tf_op jit(solution)/shard_map/ppermute | solution.py:82
  56.5 0.5 convolution_bitcast_fusion.1
  57.0 1.4 %collective-permute-done.12 = bf16[128,2,128]{2,0,1:T(8,128)(2,1)S(1)} collective-permute-done((bf16[128,2,128]{2,0,1:T(8,128)(2,1)S(1)}, bf16[128,2,128]{2,0,1:T(8,128)(2,1)S(1)}, u32[]{:S(2)}, u32[]{:S(2)}) %collective-permute-start.12) | collective-permute-done | bytes 65568 | tf_op jit(solution)/shard_map/ppermute | solution.py:82
  58.4 4.5 %collective-permute-start.13 = (bf16[128,2,128]{2,0,1:T(8,128)(2,1)S(1)}, bf16[128,2,128]{2,0,1:T(8,128)(2,1)S(1)}, u32[]{:S(2)}, u32[]{:S(2)}) collective-permute-start(bf16[128,2,128]{2,0,1:T(8,128)(2,1)S(1)} %collective-permute-done.12), channel_id=1, source_target_pairs={{0,30},{2,0},{4,2},{6,4},{8,6},{10,8},{12,10},{14,12},{16,14},{18,... | collective-permute-start | bytes 196616 | tf_op jit(solution)/shard_map/ppermute | solution.py:82
  62.9 0.0 collective-permute-done.6
  62.9 1.1 %convolution_add_fusion.1 = f32[4,128,128]{2,0,1:T(4,128)S(1)} fusion(f32[4,128,128]{2,0,1:T(4,128)S(1)} %fusion.7, f32[128,16,128]{2,0,1:T(8,128)S(1)} %convolution_bitcast_fusion.1, s32[16]{0:T(128)S(1)} %copy-done.8), kind=kOutput, calls=%fused_computation.10 | convolution fusion | flops 12648512 | bytes 1572928 | tf_op jit(solution)/shard_map/fti,tr->fri/dot_general | solution.py:17
  64.0 0.8 %collective-permute-done.13 = bf16[128,2,128]{2,0,1:T(8,128)(2,1)S(1)} collective-permute-done((bf16[128,2,128]{2,0,1:T(8,128)(2,1)S(1)}, bf16[128,2,128]{2,0,1:T(8,128)(2,1)S(1)}, u32[]{:S(2)}, u32[]{:S(2)}) %collective-permute-start.13) | collective-permute-done | bytes 65568 | tf_op jit(solution)/shard_map/ppermute | solution.py:82
  64.8 4.5 %collective-permute-start.14 = (bf16[128,2,128]{2,0,1:T(8,128)(2,1)S(1)}, bf16[128,2,128]{2,0,1:T(8,128)(2,1)S(1)}, u32[]{:S(2)}, u32[]{:S(2)}) collective-permute-start(bf16[128,2,128]{2,0,1:T(8,128)(2,1)S(1)} %collective-permute-done.13), channel_id=1, source_target_pairs={{0,30},{2,0},{4,2},{6,4},{8,6},{10,8},{12,10},{14,12},{16,14},{18,... | collective-permute-start | bytes 196616 | tf_op jit(solution)/shard_map/ppermute | solution.py:82
  69.3 0.0 collective-permute-done.7
  69.5 1.6 %collective-permute-done.14 = bf16[128,2,128]{2,0,1:T(8,128)(2,1)S(1)} collective-permute-done((bf16[128,2,128]{2,0,1:T(8,128)(2,1)S(1)}, bf16[128,2,128]{2,0,1:T(8,128)(2,1)S(1)}, u32[]{:S(2)}, u32[]{:S(2)}) %collective-permute-start.14) | collective-permute-done | bytes 65568 | tf_op jit(solution)/shard_map/ppermute | solution.py:82
  71.4 0.0 copy-start.2
  71.5 0.1 constant_dynamic-slice_fusion
  71.6 0.0 copy-start.13
  71.6 0.6 gather_fusion.1
  72.2 0.1 select_bitcast_fusion
  72.3 0.6 gather_fusion.5
  73.0 0.0 copy-start.4
  73.0 0.5 convolution_bitcast_fusion
  73.5 0.0 copy-start.5
  73.5 0.0 copy-start.9
  73.5 1.1 %fusion.3 = bf16[4,128,128]{2,0,1:T(4,128)(2,1)S(1)} fusion(f32[4,128,128]{2,0,1:T(4,128)S(1)} %convolution_add_fusion.1, f32[128,16,128]{2,0,1:T(8,128)S(1)} %convolution_bitcast_fusion, f32[4,128]{1,0:T(4,128)S(1)} %convert_bitcast_fusion, s32[16]{0:T(128)S(1)} %copy-done.13), kind=kOutput, calls=%fused_computation.16 | convolution fusion | flops 12779584 | bytes 1443904 | tf_op jit(solution)/shard_map/fti,tr->fri/dot_general | solution.py:17
  74.6 5.6 %all_gather.7 = bf16[256,512]{1,0:T(8,128)(2,1)S(1)} all-gather(bf16[128,512]{1,0:T(8,128)(2,1)S(1)} %bitcast.56), channel_id=1, replica_groups=mesh['dom'=16,'feat'=2] {'feat'}, dimensions={0}, use_global_device_ids=true | all-gather | bytes 393216 | tf_op jit(solution)/shard_map/all_gather | solution.py:102
  80.3 0.2 convolution_bitcast_fusion.3
  80.5 0.9 %fusion.4 = bf16[128,512]{1,0:T(8,128)(2,1)} fusion(f32[128,512]{1,0:T(8,128)S(1)} %convolution_bitcast_fusion.3, bf16[128,256]{1,0:T(8,128)(2,1)S(1)} %copy-done.5, bf16[256,512]{1,0:T(8,128)(2,1)S(1)} %all_gather.6, f32[128]{0:T(128)S(1)} %copy-done.9), kind=kOutput, calls=%fused_computation.17 | convolution fusion | flops 33816576 | bytes 721408 | tf_op jit(solution)/shard_map/dot_general | solution.py:95
  (75 shorter events, 0.6 us)
Async XLA Ops:
  0.0 19.1 %copy-start = (bf16[16,128,128]{2,1,0:T(8,128)(2,1)S(1)}, bf16[16,128,128]{2,1,0:T(8,128)(2,1)}, u32[]{:S(2)}) copy-start(bf16[16,128,128]{2,1,0:T(8,128)(2,1)} %param.30) | copy-start | bytes 1572868
  0.0 18.3 %copy-start.10 = (s32[16]{0:T(128)S(1)}, s32[16]{0:T(128)}, u32[]{:S(2)}) copy-start(s32[16]{0:T(128)} %param.29) | copy-start | bytes 196
  0.0 18.4 %copy-start.6 = (s32[512]{0:T(512)S(1)}, s32[512]{0:T(512)}, u32[]{:S(2)}) copy-start(s32[512]{0:T(512)} %param.23) | copy-start | bytes 6148
  5.2 15.6 %collective-permute-start = (bf16[128,2,128]{2,0,1:T(8,128)(2,1)S(1)}, bf16[128,2,128]{2,0,1:T(8,128)(2,1)S(1)}, u32[]{:S(2)}, u32[]{:S(2)}) collective-permute-start(bf16[128,2,128]{2,0,1:T(8,128)(2,1)S(1)} %copy.61), channel_id=1, source_target_pairs={{0,2},{2,4},{4,6},{6,8},{8,10},{10,12},{12,14},{14,16},{16,18},{18... | collective-permute-start | bytes 196616 | tf_op jit(solution)/shard_map/ppermute | solution.py:79
  5.7 21.6 %collective-permute-start.8 = (bf16[128,2,128]{2,0,1:T(8,128)(2,1)S(1)}, bf16[128,2,128]{2,0,1:T(8,128)(2,1)S(1)}, u32[]{:S(2)}, u32[]{:S(2)}) collective-permute-start(bf16[128,2,128]{2,0,1:T(8,128)(2,1)S(1)} %copy.61), channel_id=1, source_target_pairs={{0,30},{2,0},{4,2},{6,4},{8,6},{10,8},{12,10},{14,12},{16,14},{18,... | collective-permute-start | bytes 196616 | tf_op jit(solution)/shard_map/ppermute | solution.py:82
  12.2 7.5 %copy-start.7 = (s32[16]{0:T(128)S(1)}, s32[16]{0:T(128)}, u32[]{:S(2)}) copy-start(s32[16]{0:T(128)} %param.28) | copy-start | bytes 196
  14.6 37.4 %all-to-all-start = ((bf16[128,16,16]{0,2,1:T(8,128)(2,1)}), bf16[128,16,16]{0,2,1:T(8,128)(2,1)S(1)}, u32[]{:S(2)}, u32[]{:S(2)}) async-start(bf16[128,16,16]{0,2,1:T(8,128)(2,1)} %broadcast_multiply_fusion), calls=%async_computation | async-start | bytes 131072 | tf_op jit(solution)/shard_map/all_to_all | solution.py:53
  18.4 2.3 %copy-start.11 = (s32[16]{0:T(128)S(1)}, s32[16]{0:T(128)}, u32[]{:S(2)}) copy-start(s32[16]{0:T(128)} %param.35) | copy-start | bytes 196
  18.4 2.8 %copy-start.12 = (s32[16]{0:T(128)S(1)}, s32[16]{0:T(128)}, u32[]{:S(2)}) copy-start(s32[16]{0:T(128)} %param.32) | copy-start | bytes 196
  18.5 28.0 %copy-start.3 = (bf16[128,512]{1,0:T(8,128)(2,1)S(1)}, bf16[128,512]{1,0:T(8,128)(2,1)}, u32[]{:S(2)}) copy-start(bf16[128,512]{1,0:T(8,128)(2,1)} %param.22) | copy-start | bytes 393220
  19.1 37.4 %copy-start.1 = (bf16[16,128,128]{2,1,0:T(8,128)(2,1)S(1)}, bf16[16,128,128]{2,1,0:T(8,128)(2,1)}, u32[]{:S(2)}) copy-start(bf16[16,128,128]{2,1,0:T(8,128)(2,1)} %param.33) | copy-start | bytes 1572868
  20.8 42.1 %copy-start.8 = (s32[16]{0:T(128)S(1)}, s32[16]{0:T(128)}, u32[]{:S(2)}) copy-start(s32[16]{0:T(128)} %param.31) | copy-start | bytes 196
  20.8 6.4 %collective-permute-start.1 = (bf16[128,2,128]{2,0,1:T(8,128)(2,1)S(1)}, bf16[128,2,128]{2,0,1:T(8,128)(2,1)S(1)}, u32[]{:S(2)}, u32[]{:S(2)}) collective-permute-start(bf16[128,2,128]{2,0,1:T(8,128)(2,1)S(1)} %collective-permute-done), channel_id=1, source_target_pairs={{0,2},{2,4},{4,6},{6,8},{8,10},{10,12},{12,14},{14,16},{16,18},{18... | collective-permute-start | bytes 196616 | tf_op jit(solution)/shard_map/ppermute | solution.py:79
  27.2 6.4 %collective-permute-start.2 = (bf16[128,2,128]{2,0,1:T(8,128)(2,1)S(1)}, bf16[128,2,128]{2,0,1:T(8,128)(2,1)S(1)}, u32[]{:S(2)}, u32[]{:S(2)}) collective-permute-start(bf16[128,2,128]{2,0,1:T(8,128)(2,1)S(1)} %collective-permute-done.1), channel_id=1, source_target_pairs={{0,2},{2,4},{4,6},{6,8},{8,10},{10,12},{12,14},{14,16},{16,18},{18... | collective-permute-start | bytes 196616 | tf_op jit(solution)/shard_map/ppermute | solution.py:79
  27.3 6.4 %collective-permute-start.9 = (bf16[128,2,128]{2,0,1:T(8,128)(2,1)S(1)}, bf16[128,2,128]{2,0,1:T(8,128)(2,1)S(1)}, u32[]{:S(2)}, u32[]{:S(2)}) collective-permute-start(bf16[128,2,128]{2,0,1:T(8,128)(2,1)S(1)} %collective-permute-done.8), channel_id=1, source_target_pairs={{0,30},{2,0},{4,2},{6,4},{8,6},{10,8},{12,10},{14,12},{16,14},{18,... | collective-permute-start | bytes 196616 | tf_op jit(solution)/shard_map/ppermute | solution.py:82
  33.6 6.4 %collective-permute-start.3 = (bf16[128,2,128]{2,0,1:T(8,128)(2,1)S(1)}, bf16[128,2,128]{2,0,1:T(8,128)(2,1)S(1)}, u32[]{:S(2)}, u32[]{:S(2)}) collective-permute-start(bf16[128,2,128]{2,0,1:T(8,128)(2,1)S(1)} %collective-permute-done.2), channel_id=1, source_target_pairs={{0,2},{2,4},{4,6},{6,8},{8,10},{10,12},{12,14},{14,16},{16,18},{18... | collective-permute-start | bytes 196616 | tf_op jit(solution)/shard_map/ppermute | solution.py:79
  33.7 6.4 %collective-permute-start.10 = (bf16[128,2,128]{2,0,1:T(8,128)(2,1)S(1)}, bf16[128,2,128]{2,0,1:T(8,128)(2,1)S(1)}, u32[]{:S(2)}, u32[]{:S(2)}) collective-permute-start(bf16[128,2,128]{2,0,1:T(8,128)(2,1)S(1)} %collective-permute-done.9), channel_id=1, source_target_pairs={{0,30},{2,0},{4,2},{6,4},{8,6},{10,8},{12,10},{14,12},{16,14},{18,... | collective-permute-start | bytes 196616 | tf_op jit(solution)/shard_map/ppermute | solution.py:82
  40.0 6.4 %collective-permute-start.4 = (bf16[128,2,128]{2,0,1:T(8,128)(2,1)S(1)}, bf16[128,2,128]{2,0,1:T(8,128)(2,1)S(1)}, u32[]{:S(2)}, u32[]{:S(2)}) collective-permute-start(bf16[128,2,128]{2,0,1:T(8,128)(2,1)S(1)} %collective-permute-done.3), channel_id=1, source_target_pairs={{0,2},{2,4},{4,6},{6,8},{8,10},{10,12},{12,14},{14,16},{16,18},{18... | collective-permute-start | bytes 196616 | tf_op jit(solution)/shard_map/ppermute | solution.py:79
  40.0 12.8 %collective-permute-start.11 = (bf16[128,2,128]{2,0,1:T(8,128)(2,1)S(1)}, bf16[128,2,128]{2,0,1:T(8,128)(2,1)S(1)}, u32[]{:S(2)}, u32[]{:S(2)}) collective-permute-start(bf16[128,2,128]{2,0,1:T(8,128)(2,1)S(1)} %collective-permute-done.10), channel_id=1, source_target_pairs={{0,30},{2,0},{4,2},{6,4},{8,6},{10,8},{12,10},{14,12},{16,14},{18,... | collective-permute-start | bytes 196616 | tf_op jit(solution)/shard_map/ppermute | solution.py:82
  46.4 10.1 %collective-permute-start.5 = (bf16[128,2,128]{2,0,1:T(8,128)(2,1)S(1)}, bf16[128,2,128]{2,0,1:T(8,128)(2,1)S(1)}, u32[]{:S(2)}, u32[]{:S(2)}) collective-permute-start(bf16[128,2,128]{2,0,1:T(8,128)(2,1)S(1)} %collective-permute-done.4), channel_id=1, source_target_pairs={{0,2},{2,4},{4,6},{6,8},{8,10},{10,12},{12,14},{14,16},{16,18},{18... | collective-permute-start | bytes 196616 | tf_op jit(solution)/shard_map/ppermute | solution.py:79
  52.9 5.5 %collective-permute-start.12 = (bf16[128,2,128]{2,0,1:T(8,128)(2,1)S(1)}, bf16[128,2,128]{2,0,1:T(8,128)(2,1)S(1)}, u32[]{:S(2)}, u32[]{:S(2)}) collective-permute-start(bf16[128,2,128]{2,0,1:T(8,128)(2,1)S(1)} %collective-permute-done.11), channel_id=1, source_target_pairs={{0,30},{2,0},{4,2},{6,4},{8,6},{10,8},{12,10},{14,12},{16,14},{18,... | collective-permute-start | bytes 196616 | tf_op jit(solution)/shard_map/ppermute | solution.py:82
  56.5 6.4 %collective-permute-start.6 = (bf16[128,2,128]{2,0,1:T(8,128)(2,1)S(1)}, bf16[128,2,128]{2,0,1:T(8,128)(2,1)S(1)}, u32[]{:S(2)}, u32[]{:S(2)}) collective-permute-start(bf16[128,2,128]{2,0,1:T(8,128)(2,1)S(1)} %collective-permute-done.5), channel_id=1, source_target_pairs={{0,2},{2,4},{4,6},{6,8},{8,10},{10,12},{12,14},{14,16},{16,18},{18... | collective-permute-start | bytes 196616 | tf_op jit(solution)/shard_map/ppermute | solution.py:79
  58.4 6.4 %collective-permute-start.13 = (bf16[128,2,128]{2,0,1:T(8,128)(2,1)S(1)}, bf16[128,2,128]{2,0,1:T(8,128)(2,1)S(1)}, u32[]{:S(2)}, u32[]{:S(2)}) collective-permute-start(bf16[128,2,128]{2,0,1:T(8,128)(2,1)S(1)} %collective-permute-done.12), channel_id=1, source_target_pairs={{0,30},{2,0},{4,2},{6,4},{8,6},{10,8},{12,10},{14,12},{16,14},{18,... | collective-permute-start | bytes 196616 | tf_op jit(solution)/shard_map/ppermute | solution.py:82
  62.9 6.4 %collective-permute-start.7 = (bf16[128,2,128]{2,0,1:T(8,128)(2,1)S(1)}, bf16[128,2,128]{2,0,1:T(8,128)(2,1)S(1)}, u32[]{:S(2)}, u32[]{:S(2)}) collective-permute-start(bf16[128,2,128]{2,0,1:T(8,128)(2,1)S(1)} %collective-permute-done.6), channel_id=1, source_target_pairs={{0,2},{2,4},{4,6},{6,8},{8,10},{10,12},{12,14},{14,16},{16,18},{18... | collective-permute-start | bytes 196616 | tf_op jit(solution)/shard_map/ppermute | solution.py:79
  64.8 6.4 %collective-permute-start.14 = (bf16[128,2,128]{2,0,1:T(8,128)(2,1)S(1)}, bf16[128,2,128]{2,0,1:T(8,128)(2,1)S(1)}, u32[]{:S(2)}, u32[]{:S(2)}) collective-permute-start(bf16[128,2,128]{2,0,1:T(8,128)(2,1)S(1)} %collective-permute-done.13), channel_id=1, source_target_pairs={{0,30},{2,0},{4,2},{6,4},{8,6},{10,8},{12,10},{14,12},{16,14},{18,... | collective-permute-start | bytes 196616 | tf_op jit(solution)/shard_map/ppermute | solution.py:82
  71.4 1.5 %copy-start.2 = (bf16[16,128,128]{2,1,0:T(8,128)(2,1)S(1)}, bf16[16,128,128]{2,1,0:T(8,128)(2,1)}, u32[]{:S(2)}) copy-start(bf16[16,128,128]{2,1,0:T(8,128)(2,1)} %param.36) | copy-start | bytes 1572868
  71.6 1.9 %copy-start.13 = (s32[16]{0:T(128)S(1)}, s32[16]{0:T(128)}, u32[]{:S(2)}) copy-start(s32[16]{0:T(128)} %param.34) | copy-start | bytes 196
  73.0 7.3 %copy-start.4 = (bf16[128,256]{1,0:T(8,128)(2,1)S(1)}, bf16[128,256]{1,0:T(8,128)(2,1)}, u32[]{:S(2)}) copy-start(bf16[128,256]{1,0:T(8,128)(2,1)} %param.38) | copy-start | bytes 196612
  73.5 7.0 %copy-start.5 = (bf16[128,256]{1,0:T(8,128)(2,1)S(1)}, bf16[128,256]{1,0:T(8,128)(2,1)}, u32[]{:S(2)}) copy-start(bf16[128,256]{1,0:T(8,128)(2,1)} %param.37) | copy-start | bytes 196612
  73.5 7.0 %copy-start.9 = (f32[128]{0:T(128)S(1)}, f32[128]{0:T(128)}, u32[]{:S(2)}) copy-start(f32[128]{0:T(128)} %param.39) | copy-start | bytes 1540
